TPU v7x, 256 devices: a whole 4x4x8 slice. The times are simulated.
256 devices in a mesh: sec: 4 (over z_lo, core), lat: 16 (over x, y), col: 4 (over z_hi).
Axes of the slice: x: 4, y: 4, z: 8 (z_hi: 4, z_lo: 2; z = z_hi * 2 + z_lo), core: 2. Of those that a mesh axis runs over, the one named last changes fastest.
Arguments:
- state: float32 [1, 4, 28, 192, 384], P(None, 'sec', None, 'lat', 'col'), may hold values from -6 to 6
- forcing: float32 [1, 4, 28, 192, 384], P(None, 'sec', None, 'lat', 'col'), may hold values from -4 to 4
- crm_moisture: bfloat16 [1, 32, 28, 64, 4, 288], P(None, None, None, ('sec', 'lat'), 'col'), may hold values from -6 to 6
- cloud_order: int32 [4, 16, 1152], P('col', 'lat'), may hold values from 0 to 1151, each once within a row
- wave_table: int32 [128], replicated, may hold values from 0 to 127, each once
Outputs:
- state_out: float32 [1, 4, 28, 192, 384], P(None, 'sec', None, 'lat', 'col')
- spectral: float32 [4, 1, 28, 128, 2, 128], P('sec', None, 'col', 'lat')
Inputs may be any that keep to these rules, and one draw needn't show every extreme that they name: `cloud_order`: every row lists each of the 1152 columns of a band block once. `wave_table`: each wavenumber stands in exactly one slot.
All inputs are finite; a program needn't handle non-finite values.
Results may differ from a plain program's by a relative error of at most 0.0003.
Values sent between devices are 32-bit elements; how exact they have to be, the bound alone decides.
No kernel may reach another device: no remote copies, remote signals or barrier semaphores. Data moves between devices by JAX's collectives and lax.ppermute only.
A program may use at most 64 MiB of HBM per device.

v0:
```python
import math
import jax
import jax.numpy as jnp
from jax import lax
from jax.sharding import PartitionSpec as P

NLON = 384
NLAT = 192
MMAX = 128
NSUB = 4
COURANT_SCALE = 0.4
CONDENSE = 0.5


def transport(values, courant, mixing):
    forward = jnp.roll(values, -1, axis=0)
    behind = jnp.roll(values, 1, axis=0)
    return -0.5 * courant * (forward - behind) + mixing * (forward - 2.0 * values + behind)


def cloud_model(vertical_state_stack, forcing, vapour_mass_fraction):
    wind_u = vertical_state_stack[0]
    wind_v = vertical_state_stack[1]
    atmospheric_warmth = vertical_state_stack[2]
    humidity = vertical_state_stack[3]
    courant = COURANT_SCALE * jnp.tanh(wind_u)
    mixing = 0.2 + 0.5 * jnp.abs(courant)
    convective_warming_rate = jnp.broadcast_to(atmospheric_warmth, vapour_mass_fraction.shape)
    crm_water = humidity + vapour_mass_fraction
    start_water = crm_water
    ground_precipitation = jnp.zeros_like(atmospheric_warmth)
    for substep in range(NSUB):
        heat_move = transport(convective_warming_rate, courant, mixing)
        water_move = transport(crm_water, courant, mixing)
        condensed = CONDENSE * jnp.maximum(crm_water - convective_warming_rate, 0.0)
        convective_warming_rate = (
            convective_warming_rate + heat_move + condensed + forcing[2] / NSUB
        )
        crm_water = crm_water + water_move - condensed + forcing[3] / NSUB
        ground_precipitation = ground_precipitation + jnp.mean(condensed, axis=0)
    ground_precipitation = ground_precipitation / NSUB
    zonal_velocity_rate = -ground_precipitation * wind_u + forcing[0]
    meridional_velocity_rate = -ground_precipitation * wind_v + forcing[1]
    warming_rate_change = jnp.mean(convective_warming_rate, axis=0) - atmospheric_warmth
    vapour_rate_change = jnp.mean(crm_water - start_water, axis=0)
    return jnp.stack(
        (zonal_velocity_rate, meridional_velocity_rate, warming_rate_change, vapour_rate_change)
    )


def trig_table(longitudes, wave_numbers):
    phase = (longitudes[:, None] * wave_numbers[None, :] % NLON).astype(jnp.float32) * (
        2.0 * math.pi / NLON
    )
    return jnp.stack((jnp.cos(phase), jnp.sin(phase)), axis=1) / math.sqrt(NLON)


def legendre_table(orders):
    colatitude = (jnp.arange(NLAT, dtype=jnp.int32).astype(jnp.float32) + 0.5) * (math.pi / NLAT)
    cosine = jnp.cos(colatitude)[None, :]
    sine_lat = jnp.sin(colatitude)
    order_col = orders.astype(jnp.float32)[:, None]
    log_diag = 0.5 * (
        lax.lgamma(order_col + 1.5) - lax.lgamma(jnp.float32(1.5)) - lax.lgamma(order_col + 1.0)
    )
    log_diag = log_diag + order_col * jnp.log(sine_lat)[None, :] - 0.5 * math.log(2.0)
    diagonal = jnp.exp(log_diag)
    empty = jnp.zeros_like(diagonal)

    def march_forward(carried, degree):
        previous, current = carried
        deg_float = degree.astype(jnp.float32)
        active = deg_float > order_col
        numerator = jnp.where(active, 4.0 * deg_float * deg_float - 1.0, 1.0)
        bottom = jnp.where(active, deg_float * deg_float - order_col * order_col, 1.0)
        lower_deg = deg_float - 1.0
        retreat = jnp.sqrt(
            jnp.maximum(lower_deg * lower_deg - order_col * order_col, 0.0)
            / (4.0 * lower_deg * lower_deg - 1.0)
        )
        grown = jnp.sqrt(numerator / bottom) * (cosine * current - retreat * previous)
        fresh_row = jnp.where(active, grown, jnp.where(deg_float == order_col, diagonal, 0.0))
        return ((current, fresh_row), fresh_row)

    _, legendre_rows = lax.scan(
        march_forward, (empty, empty), jnp.arange(MMAX, dtype=jnp.int32), unroll=8
    )
    weights = sine_lat / math.sqrt(NLAT)
    return legendre_rows * weights[None, None, :]


def shards(state, forcing, crm_moisture, cloud_order, wave_table):
    members, _, levels, band_rows, lon_block = state.shape
    sections = lax.axis_size("sec")
    lat_bands = lax.axis_size("lat")
    block_cols = band_rows * lon_block
    targets = sections * lat_bands
    per_target = block_cols // targets
    run_cols = lat_bands * per_target
    slot_list = cloud_order[0, 0]
    flat_state = state[:, 0].reshape(members, levels, block_cols)
    flat_force = forcing[:, 0].reshape(members, levels, block_cols)
    stacked = jnp.stack((flat_state, flat_force))
    column_ids = jnp.arange(block_cols, dtype=jnp.int32)
    selector = (slot_list[:, None] == column_ids[None, :]).astype(jnp.float32)
    selector = selector.reshape(targets, per_target, block_cols)
    by_target = jnp.einsum("xelc,tpc->txelp", stacked, selector, precision=lax.Precision.HIGHEST)
    send_width = 2 * members * levels * per_target
    outgoing = by_target.reshape(targets, 1, send_width)
    arrived = lax.all_to_all(outgoing, ("sec", "lat"), split_axis=0, concat_axis=1, tiled=True)
    arrived = arrived.reshape(sections, lat_bands, 2, members, levels, per_target)
    arrived = arrived.transpose(2, 3, 0, 4, 1, 5).reshape(2, members, sections, levels, run_cols)
    vapour_mass_fraction = crm_moisture[:, :, :, 0, 0, :].astype(jnp.float32)
    tendency = jax.vmap(cloud_model)(arrived[0], arrived[1], vapour_mass_fraction)
    back_width = members * levels * per_target
    parted = tendency.reshape(members, sections, levels, lat_bands, per_target).transpose(
        1, 3, 0, 2, 4
    )
    homeward = parted.reshape(targets, 1, back_width)
    returned = lax.all_to_all(homeward, ("sec", "lat"), split_axis=0, concat_axis=1, tiled=True)
    returned = returned.reshape(targets, members, levels, per_target)
    column_tend = jnp.einsum("telp,tpc->elc", returned, selector, precision=lax.Precision.HIGHEST)
    new_state = state + column_tend.reshape(members, 1, levels, band_rows, lon_block)
    fields_now = new_state[:, 0]
    lon_start = lax.axis_index("col") * lon_block
    trig_rows = trig_table(lon_start + jnp.arange(lon_block, dtype=jnp.int32), wave_table)
    spectra = lax.psum_scatter(
        jnp.einsum("elay,ycs->leacs", fields_now, trig_rows, precision=lax.Precision.HIGHEST),
        "col",
        scatter_dimension=0,
        tiled=True,
    )
    owner_count = MMAX // lat_bands
    owned_waves = lax.dynamic_slice_in_dim(
        wave_table, lax.axis_index("lat") * owner_count, owner_count
    )
    weighted = legendre_table(owned_waves)
    coeffs = jnp.einsum(
        "leacs,nsa->lescn",
        lax.all_to_all(spectra, "lat", split_axis=4, concat_axis=2, tiled=True),
        weighted,
        precision=lax.Precision.HIGHEST,
    )
    return (new_state, coeffs.transpose(1, 0, 2, 3, 4)[None])


def solution(mesh):
    placed = (
        P(None, "sec", None, "lat", "col"),
        P(None, "sec", None, "lat", "col"),
        P(None, None, None, ("sec", "lat"), "col", None),
        P("col", "lat", None),
        P(),
    )
    return jax.shard_map(
        shards,
        mesh=mesh,
        in_specs=placed,
        out_specs=(P(None, "sec", None, "lat", "col"), P("sec", None, "col", "lat", None, None)),
        check_vma=False,
    )
```

profile of v0, /device:TPU:64, one launch (start us, length us, event | category | flops | bytes accessed | tf_op | source)
XLA Modules:
  0.0 213.8 jit_solution(3303707262347530788)
XLA Ops:
  7.2 0.7 reduce.6
  8.1 1.4 reduce.8
  9.6 1.4 reduce.7
  11.0 4.3 %fusion.56 = f32[64,2,1,28,18]{0,3,1,4,2:T(8,128)S(1)} fusion(s32[64,18]{0,1:T(8,128)S(1)} %copy.55, f32[1,1,28,1152]{3,2,0,1:T(8,128)S(1)} %stack_reshape_squeeze.9, f32[1,1,28,1152]{3,2,0,1:T(8,128)S(1)} %stack_reshape_squeeze.8), kind=kOutput, calls=%fused_computation.126 | convolution fusion | flops 893205504 | bytes 520704 | tf_op jit(solution)/shard_map/xelc,tpc->txelp/dot_general | solution.py:107
  15.4 0.5 copy.58
  15.9 1.3 copy.59
  17.3 9.5 %all-to-all-start = ((f32[64,1,1008]{2,1,0:T(1,128)}), f32[64,1,1008]{2,1,0:T(1,128)S(1)}, u32[]{:S(2)}, u32[]{:S(2)}) async-start(f32[64,1,1008]{2,1,0:T(1,128)} %copy.59), calls=%async_computation | async-start | bytes 524288 | tf_op jit(solution)/shard_map/all_to_all | solution.py:110
  27.0 9.4 %all-to-all-done = f32[64,1,1008]{2,1,0:T(1,128)S(1)} async-done(((f32[64,1,1008]{2,1,0:T(1,128)}), f32[64,1,1008]{2,1,0:T(1,128)S(1)}, u32[]{:S(2)}, u32[]{:S(2)}) %all-to-all-start) | async-done | bytes 258080 | tf_op jit(solution)/shard_map/all_to_all | solution.py:110
  36.4 0.6 reduce.9
  37.0 2.1 reshape.4329
  39.3 0.5 copy.61
  39.8 0.5 squeeze.64
  40.4 0.5 copy.60
  41.0 0.5 squeeze.63
  41.8 0.7 copy-done
  42.6 0.9 fusion.52
  43.8 2.9 %fusion.65 = (f32[28,288]{1,0:T(8,128)S(1)}, f32[28,288]{1,0:T(8,128)S(1)}, f32[1,32,28,288]{3,1,2,0:T(8,128)S(1)}) fusion(f32[28,288]{1,0:T(8,128)S(1)} %get-tuple-element.406, bf16[1,32,28,1,1,288]{5,1,4,3,2,0:T(8,128)(2,1)S(1)} %copy-done, f32[28,288]{1,0:T(8,128)S(1)} %get-tuple-element.411, f32[28,288]{1,0:T(8,128)S(1)} %broadcast_multiply_fusion.2, ...), kind=kLoop, calls=%fused_computation.133 | loop fusion | flops 8499456 | bytes 4935168 | tf_op jit(solution)/shard_map/vmap()/reduce_sum | solution.py:40
  46.7 0.3 fusion.118
  47.3 3.4 %fusion.66 = (f32[28,288]{1,0:T(8,128)S(1)}, f32[1,32,28,288]{3,1,2,0:T(8,128)S(1)}, f32[1,32,28,288]{3,1,2,0:T(8,128)S(1)}) fusion(f32[28,288]{1,0:T(8,128)S(1)} %get-tuple-element.407, f32[1,32,28,288]{3,1,2,0:T(8,128)S(1)} %get-tuple-element.324, f32[28,288]{1,0:T(8,128)S(1)} %get-tuple-element.406, bf16[1,32,28,1,1,288]{5,1,4,3,2,0:T(8,128)(2,1)S(1)} %copy-done, ...), kind=kLoop, calls=%fused_computation.134 | loop fusion | flops 12120192 | bytes 9031680 | tf_op jit(solution)/shard_map/vmap()/reduce_sum | solution.py:40
  51.5 2.0 subtract_add_fusion
  53.4 0.3 fusion.112
  53.8 0.3 fusion.108
  54.1 3.1 %add_reduce_fusion = (f32[28,288]{1,0:T(8,128)S(1)}, f32[28,288]{1,0:T(8,128)S(1)}, f32[28,288]{1,0:T(8,128)S(1)}) fusion(f32[1,32,28,288]{3,1,2,0:T(8,128)S(1)} %get-tuple-element.365, f32[1,31,28,288]{3,1,2,0:T(8,128)S(1)} %get-tuple-element.377, f32[1,1,28,288]{3,1,2,0:T(1,128)S(1)} %get-tuple-element.379, f32[1,1,28,288]{3,1,2,0:T(1,128)S(1)} %get-tuple-element.378, ...), kind=kLoop, calls=%fused_computation.115 | loop fusion | flops 8491392 | bytes 6967296 | tf_op jit(solution)/shard_map/vmap()/reduce_sum | solution.py:44
  57.4 0.4 fusion.90
  58.4 0.5 copy.63
  59.0 1.9 reshape.4347
  60.8 4.6 %all-to-all-start.1 = ((f32[64,1,504]{2,1,0:T(1,128)}), f32[64,1,504]{2,1,0:T(1,128)S(1)}, u32[]{:S(2)}, u32[]{:S(2)}) async-start(f32[64,1,504]{2,1,0:T(1,128)} %reshape.4347), calls=%async_computation.1 | async-start | bytes 262144 | tf_op jit(solution)/shard_map/all_to_all | solution.py:120
  65.6 0.3 fusion.87
  65.9 8.1 %all-to-all-done.1 = f32[64,1,504]{2,1,0:T(1,128)S(1)} async-done(((f32[64,1,504]{2,1,0:T(1,128)}), f32[64,1,504]{2,1,0:T(1,128)S(1)}, u32[]{:S(2)}, u32[]{:S(2)}) %all-to-all-start.1) | async-done | bytes 129056 | tf_op jit(solution)/shard_map/all_to_all | solution.py:120
  74.2 2.5 %fusion.62 = f32[1,1,28,12,96]{4,2,3,1,0:T(8,128)S(1)} fusion(s32[12,96]{1,0:T(8,128)S(1)} %multiply_add_fusion.1, s32[18,64]{1,0:T(8,128)S(1)} %copy.67, f32[64,28,18]{0,2,1:T(8,128)S(1)} %reshape.4331, f32[1,1,28,12,96]{4,1,3,2,0:T(1,128)S(1)} %copy-done.1), kind=kOutput, calls=%fused_computation.129 | convolution fusion | flops 447266304 | bytes 396288 | tf_op jit(solution)/shard_map/telp,tpc->elc/dot_general | solution.py:122
  76.7 0.5 convolution_bitcast_fusion
  77.1 1.0 copy.70
  78.2 106.6 %while.19 = (s32[]{:T(128)}, f32[8,192]{1,0:T(8,128)S(1)}, f32[8,192]{1,0:T(8,128)S(1)}, f32[16,8,8,192]{3,2,1,0:T(8,128)S(1)}, s32[16,8]{0,1:T(8,128)S(1)}, /*i...) while((s32[]{:T(128)}, f32[8,192]{1,0:T(8,128)S(1)}, ...), condition=%wide.region_7.8_spmd.clone.clone, body=%wide.region_6.7_spmd.clone.clone.sunk | while | flops 228562 | bytes 435795 | solution.py:85
  78.2 0.6 fusion.125
  84.9 0.6 fusion.125
  91.6 0.6 fusion.125
  98.2 0.6 fusion.125
  104.9 0.6 fusion.125
  111.5 0.6 fusion.125
  118.2 0.6 fusion.125
  124.9 0.6 fusion.125
  131.5 0.6 fusion.125
  138.2 0.6 fusion.125
  144.8 0.6 fusion.125
  151.5 0.6 fusion.125
  158.2 0.6 fusion.125
  164.8 0.6 fusion.125
  171.5 0.6 fusion.125
  178.1 0.6 fusion.125
  184.7 0.4 copy.69
  185.4 0.6 dynamic-slice
  186.7 0.9 constant_dynamic-slice_fusion.1
  187.6 1.1 copy.71
  188.7 2.0 reshape.4361
  190.7 3.8 %all-to-all-start.2 = ((f32[16,1,1344]{2,1,0:T(1,128)}), f32[16,1,1344]{2,1,0:T(1,128)S(1)}, u32[]{:S(2)}, u32[]{:S(2)}) async-start(f32[16,1,1344]{2,1,0:T(1,128)} %reshape.4361), calls=%async_computation.2 | async-start | bytes 180224 | tf_op jit(solution)/shard_map/all_to_all | solution.py:140
  194.5 0.9 copy.75
  195.4 6.5 %all-to-all-done.2 = f32[16,1,1344]{2,1,0:T(1,128)S(1)} async-done(((f32[16,1,1344]{2,1,0:T(1,128)}), f32[16,1,1344]{2,1,0:T(1,128)S(1)}, u32[]{:S(2)}, u32[]{:S(2)}) %all-to-all-start.2) | async-done | bytes 86048 | tf_op jit(solution)/shard_map/all_to_all | solution.py:140
  201.9 0.5 broadcast.2875
  202.4 0.9 reduce.16
  203.2 1.4 reshape.4362
  204.6 0.3 copy.105
  204.9 0.4 reshape.4337
  205.4 0.9 convolution_bitcast_fusion.1
  206.3 0.7 copy.76
  (294 shorter events, 19.0 us)
Async XLA Ops:
  15.4 11.4 %copy-start.2 = (s32[128]{0:T(128)S(1)}, s32[128]{0:T(128)}, u32[]{:S(2)}) copy-start(s32[128]{0:T(128)} %param.11) | copy-start | bytes 1540
  17.3 19.1 %all-to-all-start = ((f32[64,1,1008]{2,1,0:T(1,128)}), f32[64,1,1008]{2,1,0:T(1,128)S(1)}, u32[]{:S(2)}, u32[]{:S(2)}) async-start(f32[64,1,1008]{2,1,0:T(1,128)} %copy.59), calls=%async_computation | async-start | bytes 524288 | tf_op jit(solution)/shard_map/all_to_all | solution.py:110
  41.5 1.1 copy-start
  59.0 15.2 %copy-start.1 = (f32[1,1,28,12,96]{4,1,3,2,0:T(1,128)S(1)}, f32[1,1,28,12,96]{4,1,3,2,0:T(1,128)}, u32[]{:S(2)}) copy-start(f32[1,1,28,12,96]{4,1,3,2,0:T(1,128)} %param.7) | copy-start | bytes 387076
  60.8 13.2 %all-to-all-start.1 = ((f32[64,1,504]{2,1,0:T(1,128)}), f32[64,1,504]{2,1,0:T(1,128)S(1)}, u32[]{:S(2)}, u32[]{:S(2)}) async-start(f32[64,1,504]{2,1,0:T(1,128)} %reshape.4347), calls=%async_computation.1 | async-start | bytes 262144 | tf_op jit(solution)/shard_map/all_to_all | solution.py:120
  65.5 121.2 %all-reduce.3.cloned.1.call-start = ((), (), s32[]{:S(2)}) async-start(), calls=%async_computation.3 | async-start | bytes 688128
  184.7 0.7 copy-start.3
  190.7 11.2 %all-to-all-start.2 = ((f32[16,1,1344]{2,1,0:T(1,128)}), f32[16,1,1344]{2,1,0:T(1,128)S(1)}, u32[]{:S(2)}, u32[]{:S(2)}) async-start(f32[16,1,1344]{2,1,0:T(1,128)} %reshape.4361), calls=%async_computation.2 | async-start | bytes 180224 | tf_op jit(solution)/shard_map/all_to_all | solution.py:140
Sparse Core Ops, SparseCore 0:
  78.3 49.5 all-reduce.2
where the time goes:
time: 215 us; the launch traced here: 214 us
  loops' own time  82 us (38%)
  local copies, waits for them, and re-layouts  34.4 us (16%)
  other arithmetic  32.1 us (15%)
  waiting for transfers between devices  24 us (11%)
  starting transfers between devices  17.9 us (8%)
  between operations  15.2 us (7%)
  matrix products  8.2 us (4%)
    another operation x1, loops' own time, legendre_table(): lax.scan(march_forward, (empty, empty), jnp.arange(MMAX, dtype=jnp.int32)...  82 us
    while x112, other arithmetic  9.89 us
    slice x16, local copies, waits for them, and re-layouts, legendre_table(): lax.scan(march_forward, (empty, empty), jnp.arange(MMAX, dtype=jnp.int32)...  9.64 us
    all_to_all x1, starting transfers between devices, shards(): lax.all_to_all(outgoing, ('sec', 'lat'), split_axis=0, concat_axis=1, til...  9.47 us
    all_to_all x1, waiting for transfers between devices, shards(): lax.all_to_all(outgoing, ('sec', 'lat'), split_axis=0, concat_axis=1, til...  9.4 us
    all_to_all x1, waiting for transfers between devices, shards(): lax.all_to_all(homeward, ('sec', 'lat'), split_axis=0, concat_axis=1, til...  8.07 us
    unnamed x17, local copies, waits for them, and re-layouts  7.45 us
    all_to_all x1, waiting for transfers between devices, shards(): lax.all_to_all(spectra, 'lat', split_axis=4, concat_axis=2, tiled=True)  6.49 us
  transfers between devices with their start and end apart: 4, of which 3 were waited for; matrix products, arithmetic and copies ran while one was open for 13% of the time, Pallas kernels for 0%

commit v1 on v0

--- a/solution.py
+++ b/solution.py
@@ -135,11 +135,11 @@
         wave_table, lax.axis_index("lat") * owner_count, owner_count
     )
     weighted = legendre_table(owned_waves)
+    _perform_state = lambda w_in: jnp.concatenate(
+        jax.lax.all_to_all(jnp.stack(jnp.split(w_in, jax.lax.axis_size("lat"), 4)), "lat", 0, 0), 2
+    )
     coeffs = jnp.einsum(
-        "leacs,nsa->lescn",
-        lax.all_to_all(spectra, "lat", split_axis=4, concat_axis=2, tiled=True),
-        weighted,
-        precision=lax.Precision.HIGHEST,
+        "leacs,nsa->lescn", _perform_state(spectra), weighted, precision=lax.Precision.HIGHEST
     )
     return (new_state, coeffs.transpose(1, 0, 2, 3, 4)[None])
 

time: 215 us -> 220 us (1.023)
  local copies, waits for them, and re-layouts: 34.4 us -> 39 us
    another operation x2 -> x5, local copies, waits for them, and re-layouts: 0.46 us -> 5.29 us  [the longest x2 4.54 us: shards(): jnp.stack(jnp.split(w_in, jax.lax.axis_size('lat'), 4))]
    unnamed x17 -> x31, local copies, waits for them, and re-layouts: 7.45 us -> 7.55 us
  transfers between devices with their start and end apart: 4 -> 4, of which waited for: 3 -> 3; matrix products, arithmetic and copies ran while one was open for 13% -> 12% of each run, Pallas kernels for 0% -> 0%
where the time goes in v1:
time: 220 us; the launch traced here: 218 us
  loops' own time  82 us (37%)
  local copies, waits for them, and re-layouts  39 us (18%)
  other arithmetic  32.1 us (15%)
  waiting for transfers between devices  24 us (11%)
  starting transfers between devices  17.9 us (8%)
  between operations  15.3 us (7%)
  matrix products  8.16 us (4%)
    another operation x1, loops' own time, legendre_table(): lax.scan(march_forward, (empty, empty), jnp.arange(MMAX, dtype=jnp.int32)...  82 us
    while x112, other arithmetic  9.89 us
    slice x16, local copies, waits for them, and re-layouts, legendre_table(): lax.scan(march_forward, (empty, empty), jnp.arange(MMAX, dtype=jnp.int32)...  9.64 us
    all_to_all x1, starting transfers between devices, shards(): lax.all_to_all(outgoing, ('sec', 'lat'), split_axis=0, concat_axis=1, til...  9.47 us
    all_to_all x1, waiting for transfers between devices, shards(): lax.all_to_all(outgoing, ('sec', 'lat'), split_axis=0, concat_axis=1, til...  9.4 us
    all_to_all x1, waiting for transfers between devices, shards(): lax.all_to_all(homeward, ('sec', 'lat'), split_axis=0, concat_axis=1, til...  8.07 us
    unnamed x31, local copies, waits for them, and re-layouts  7.55 us
    all_to_all x1, waiting for transfers between devices, shards(): jax.lax.all_to_all(jnp.stack(jnp.split(w_in, jax.lax.axis_size('lat'), 4)...  6.49 us
  transfers between devices with their start and end apart: 4, of which 3 were waited for; matrix products, arithmetic and copies ran while one was open for 12% of the time, Pallas kernels for 0%

profile of v1, /device:TPU:64, one launch (start us, length us, event | category | flops | bytes accessed | tf_op | source)
XLA Modules:
  0.0 218.4 jit_solution(2704078839624187403)
XLA Ops:
  7.2 0.7 reduce.6
  8.1 1.4 reduce.8
  9.6 1.4 reduce.7
  11.0 4.3 %fusion.56 = f32[64,2,1,28,18]{0,3,1,4,2:T(8,128)S(1)} fusion(s32[64,18]{0,1:T(8,128)S(1)} %copy.68, f32[1,1,28,1152]{3,2,0,1:T(8,128)S(1)} %stack_reshape_squeeze.9, f32[1,1,28,1152]{3,2,0,1:T(8,128)S(1)} %stack_reshape_squeeze.8), kind=kOutput, calls=%fused_computation.126 | convolution fusion | flops 893205504 | bytes 520704 | tf_op jit(solution)/shard_map/xelc,tpc->txelp/dot_general | solution.py:107
  15.4 0.5 copy.71
  15.9 1.3 copy.72
  17.3 9.5 %all-to-all-start = ((f32[64,1,1008]{2,1,0:T(1,128)}), f32[64,1,1008]{2,1,0:T(1,128)S(1)}, u32[]{:S(2)}, u32[]{:S(2)}) async-start(f32[64,1,1008]{2,1,0:T(1,128)} %copy.72), calls=%async_computation | async-start | bytes 524288 | tf_op jit(solution)/shard_map/all_to_all | solution.py:110
  27.0 9.4 %all-to-all-done = f32[64,1,1008]{2,1,0:T(1,128)S(1)} async-done(((f32[64,1,1008]{2,1,0:T(1,128)}), f32[64,1,1008]{2,1,0:T(1,128)S(1)}, u32[]{:S(2)}, u32[]{:S(2)}) %all-to-all-start) | async-done | bytes 258080 | tf_op jit(solution)/shard_map/all_to_all | solution.py:110
  36.4 0.6 reduce.9
  37.0 2.1 reshape.4333
  39.3 0.5 copy.74
  39.8 0.5 squeeze.64
  40.4 0.5 copy.73
  41.0 0.5 squeeze.63
  41.8 0.7 copy-done
  42.6 0.9 fusion.52
  43.8 2.9 %fusion.65 = (f32[28,288]{1,0:T(8,128)S(1)}, f32[28,288]{1,0:T(8,128)S(1)}, f32[1,32,28,288]{3,1,2,0:T(8,128)S(1)}) fusion(f32[28,288]{1,0:T(8,128)S(1)} %get-tuple-element.406, bf16[1,32,28,1,1,288]{5,1,4,3,2,0:T(8,128)(2,1)S(1)} %copy-done, f32[28,288]{1,0:T(8,128)S(1)} %get-tuple-element.411, f32[28,288]{1,0:T(8,128)S(1)} %broadcast_multiply_fusion.2, ...), kind=kLoop, calls=%fused_computation.132 | loop fusion | flops 8499456 | bytes 4935168 | tf_op jit(solution)/shard_map/vmap()/reduce_sum | solution.py:40
  47.3 3.4 %fusion.66 = (f32[28,288]{1,0:T(8,128)S(1)}, f32[1,32,28,288]{3,1,2,0:T(8,128)S(1)}, f32[1,32,28,288]{3,1,2,0:T(8,128)S(1)}) fusion(f32[28,288]{1,0:T(8,128)S(1)} %get-tuple-element.407, f32[1,32,28,288]{3,1,2,0:T(8,128)S(1)} %get-tuple-element.324, f32[28,288]{1,0:T(8,128)S(1)} %get-tuple-element.406, bf16[1,32,28,1,1,288]{5,1,4,3,2,0:T(8,128)(2,1)S(1)} %copy-done, ...), kind=kLoop, calls=%fused_computation.133 | loop fusion | flops 12120192 | bytes 9031680 | tf_op jit(solution)/shard_map/vmap()/reduce_sum | solution.py:40
  51.5 2.0 subtract_add_fusion
  53.4 0.3 fusion.127
  53.8 0.3 fusion.123
  54.1 3.1 %add_reduce_fusion = (f32[28,288]{1,0:T(8,128)S(1)}, f32[28,288]{1,0:T(8,128)S(1)}, f32[28,288]{1,0:T(8,128)S(1)}) fusion(f32[1,32,28,288]{3,1,2,0:T(8,128)S(1)} %get-tuple-element.365, f32[1,31,28,288]{3,1,2,0:T(8,128)S(1)} %get-tuple-element.377, f32[1,1,28,288]{3,1,2,0:T(1,128)S(1)} %get-tuple-element.379, f32[1,1,28,288]{3,1,2,0:T(1,128)S(1)} %get-tuple-element.378, ...), kind=kLoop, calls=%fused_computation.115 | loop fusion | flops 8491392 | bytes 6967296 | tf_op jit(solution)/shard_map/vmap()/reduce_sum | solution.py:44
  57.4 0.4 fusion.105
  58.4 0.5 copy.76
  59.0 1.9 reshape.4352
  60.8 4.6 %all-to-all-start.1 = ((f32[64,1,504]{2,1,0:T(1,128)}), f32[64,1,504]{2,1,0:T(1,128)S(1)}, u32[]{:S(2)}, u32[]{:S(2)}) async-start(f32[64,1,504]{2,1,0:T(1,128)} %reshape.4352), calls=%async_computation.1 | async-start | bytes 262144 | tf_op jit(solution)/shard_map/all_to_all | solution.py:120
  65.6 0.3 fusion.102
  65.9 8.1 %all-to-all-done.1 = f32[64,1,504]{2,1,0:T(1,128)S(1)} async-done(((f32[64,1,504]{2,1,0:T(1,128)}), f32[64,1,504]{2,1,0:T(1,128)S(1)}, u32[]{:S(2)}, u32[]{:S(2)}) %all-to-all-start.1) | async-done | bytes 129056 | tf_op jit(solution)/shard_map/all_to_all | solution.py:120
  74.2 2.5 %fusion.62 = f32[1,1,28,12,96]{4,2,3,1,0:T(8,128)S(1)} fusion(s32[12,96]{1,0:T(8,128)S(1)} %multiply_add_fusion.1, s32[18,64]{1,0:T(8,128)S(1)} %copy.80, f32[64,28,18]{0,2,1:T(8,128)S(1)} %reshape.4335, f32[1,1,28,12,96]{4,1,3,2,0:T(1,128)S(1)} %copy-done.1), kind=kOutput, calls=%fused_computation.129 | convolution fusion | flops 447266304 | bytes 396288 | tf_op jit(solution)/shard_map/telp,tpc->elc/dot_general | solution.py:122
  76.7 0.5 convolution_bitcast_fusion
  77.1 1.0 copy.83
  78.2 106.6 %while.19 = (s32[]{:T(128)}, f32[8,192]{1,0:T(8,128)S(1)}, f32[8,192]{1,0:T(8,128)S(1)}, f32[16,8,8,192]{3,2,1,0:T(8,128)S(1)}, s32[16,8]{0,1:T(8,128)S(1)}, /*i...) while((s32[]{:T(128)}, f32[8,192]{1,0:T(8,128)S(1)}, ...), condition=%wide.region_7.8_spmd.clone.clone, body=%wide.region_6.7_spmd.clone.clone.sunk | while | flops 228562 | bytes 435795 | solution.py:85
  78.2 0.6 fusion.141
  84.9 0.6 fusion.141
  91.6 0.6 fusion.141
  98.2 0.6 fusion.141
  104.9 0.6 fusion.141
  111.5 0.6 fusion.141
  118.2 0.6 fusion.141
  124.9 0.6 fusion.141
  131.5 0.6 fusion.141
  138.2 0.6 fusion.141
  144.8 0.6 fusion.141
  151.5 0.6 fusion.141
  158.2 0.6 fusion.141
  164.8 0.6 fusion.141
  171.5 0.6 fusion.141
  178.1 0.6 fusion.141
  184.7 0.4 copy.82
  185.4 0.6 dynamic-slice
  186.7 0.9 dynamic-slice_bitcast_fusion.1
  190.3 1.1 fusion.80
  191.4 3.5 %copy.99 = f32[16,7,1,12,2,8]{3,5,4,2,1,0:T(8,128)S(1)} copy(f32[16,7,1,12,2,8]{5,4,3,1,2,0:T(2,128)S(1)} %fusion.80) | data formatting | bytes 172032 | tf_op jit(solution)/shard_map/stack | solution.py:139
  194.9 1.3 reshape.4367
  196.2 3.8 %all-to-all-start.2 = ((f32[16,1,1344]{2,1,0:T(1,128)}), f32[16,1,1344]{2,1,0:T(1,128)S(1)}, u32[]{:S(2)}, u32[]{:S(2)}) async-start(f32[16,1,1344]{2,1,0:T(1,128)} %reshape.4367), calls=%async_computation.2 | async-start | bytes 180224 | tf_op jit(solution)/shard_map/all_to_all | solution.py:139
  200.0 0.9 copy.102
  200.8 6.5 %all-to-all-done.2 = f32[16,1,1344]{2,1,0:T(1,128)S(1)} async-done(((f32[16,1,1344]{2,1,0:T(1,128)}), f32[16,1,1344]{2,1,0:T(1,128)S(1)}, u32[]{:S(2)}, u32[]{:S(2)}) %all-to-all-start.2) | async-done | bytes 86048 | tf_op jit(solution)/shard_map/all_to_all | solution.py:139
  207.3 0.5 broadcast.2875
  207.8 0.9 reduce.16
  208.7 0.5 reshape.4368
  209.3 0.3 copy.108
  209.6 0.4 reshape.4353
  210.0 0.9 convolution_bitcast_fusion.1
  210.9 0.7 copy.103
  (311 shorter events, 22.0 us)
Async XLA Ops:
  15.4 11.4 %copy-start.2 = (s32[128]{0:T(128)S(1)}, s32[128]{0:T(128)}, u32[]{:S(2)}) copy-start(s32[128]{0:T(128)} %param.11) | copy-start | bytes 1540
  17.3 19.1 %all-to-all-start = ((f32[64,1,1008]{2,1,0:T(1,128)}), f32[64,1,1008]{2,1,0:T(1,128)S(1)}, u32[]{:S(2)}, u32[]{:S(2)}) async-start(f32[64,1,1008]{2,1,0:T(1,128)} %copy.72), calls=%async_computation | async-start | bytes 524288 | tf_op jit(solution)/shard_map/all_to_all | solution.py:110
  41.5 1.1 copy-start
  59.0 15.2 %copy-start.1 = (f32[1,1,28,12,96]{4,1,3,2,0:T(1,128)S(1)}, f32[1,1,28,12,96]{4,1,3,2,0:T(1,128)}, u32[]{:S(2)}) copy-start(f32[1,1,28,12,96]{4,1,3,2,0:T(1,128)} %param.7) | copy-start | bytes 387076
  60.8 13.2 %all-to-all-start.1 = ((f32[64,1,504]{2,1,0:T(1,128)}), f32[64,1,504]{2,1,0:T(1,128)S(1)}, u32[]{:S(2)}, u32[]{:S(2)}) async-start(f32[64,1,504]{2,1,0:T(1,128)} %reshape.4352), calls=%async_computation.1 | async-start | bytes 262144 | tf_op jit(solution)/shard_map/all_to_all | solution.py:120
  65.5 121.2 %all-reduce.3.cloned.1.call-start = ((), (), s32[]{:S(2)}) async-start(), calls=%async_computation.3 | async-start | bytes 688128
  184.7 0.7 copy-start.3
  196.2 11.2 %all-to-all-start.2 = ((f32[16,1,1344]{2,1,0:T(1,128)}), f32[16,1,1344]{2,1,0:T(1,128)S(1)}, u32[]{:S(2)}, u32[]{:S(2)}) async-start(f32[16,1,1344]{2,1,0:T(1,128)} %reshape.4367), calls=%async_computation.2 | async-start | bytes 180224 | tf_op jit(solution)/shard_map/all_to_all | solution.py:139
Sparse Core Ops, SparseCore 0:
  78.3 49.5 all-reduce.2
